TPU v7x, 256 devices: a whole 4x4x8 slice. The times are simulated.
256 devices in a mesh: seq: 32 (over y, x, core), head: 8 (over z).
Axes of the slice: x: 4, y: 4, z: 8, core: 2. Of those that a mesh axis runs over, the one named last changes fastest.
Arguments:
- query_rows: bfloat16 [16384, 4096], P('seq', 'head'), may hold values from -6 to 6
- key_rows: bfloat16 [16384, 4096], P('seq', 'head'), may hold values from -6 to 6
- value_rows: bfloat16 [16384, 4096], P('seq', 'head'), may hold values from -6 to 6
- out_weight: bfloat16 [4096, 4096], P('seq', 'head'), may hold values from -0.09375 to 0.09375
- target_rows: bfloat16 [16384, 4096], P('seq', 'head'), may hold values from -6 to 6
Outputs:
- output: bfloat16 [16384, 4096], P('seq', 'head')
- grad_query: bfloat16 [16384, 4096], P('seq', 'head')
- grad_key: bfloat16 [16384, 4096], P('seq', 'head')
- grad_value: bfloat16 [16384, 4096], P('seq', 'head')
- grad_weight: float32 [4096, 4096], P('seq', 'head')
All inputs are finite; a program needn't handle non-finite values.
Results may differ from a plain program's by a relative error of at most 0.019.
Values may be sent and summed in bfloat16 or wider, within the bound.
A program may use at most 64 MiB of HBM per device.

v0:
```python
import math
import jax
import jax.numpy as jnp
from jax import lax
from jax.sharding import Mesh
from jax.sharding import PartitionSpec as P

DH = 128
BLK = 512
SEQ = ("seq_0", "seq_1", "seq_2")
EXACT = lax.Precision.HIGHEST


def filled_with(x, identity):
    return jnp.broadcast_to(jnp.asarray(identity, x.dtype), x.shape)


def entering(x, axes, combine, identity, reverse):
    before = start = filled_with(x, identity)
    so_far = x
    for axis in reversed(axes):
        devices, place = (lax.axis_size(axis), lax.axis_index(axis))
        pieces = lax.all_gather(so_far.astype(jnp.bfloat16), axis)
        inside, so_far = (start, start)
        for k in reversed(range(devices)) if reverse else range(devices):
            passed = k > place if reverse else k < place
            so_far = combine(so_far, pieces[k].astype(x.dtype))
            inside = jnp.where(passed, so_far, inside)
        before = combine(inside, before)
    return before


def add_states(earlier, later_one):
    return earlier + later_one


def on_device(query_rows, key_rows, value_rows, out_weight, target_rows):
    rows_dev = query_rows.shape[0]
    feature_width = query_rows.shape[1]
    local_heads = feature_width // DH
    block_count = rows_dev // BLK
    seq_count = lax.axis_size(SEQ)
    total_rows = rows_dev * seq_count
    seq_index = lax.axis_index(SEQ)
    positions = (seq_index * rows_dev + jnp.arange(rows_dev, dtype=jnp.int32) + 1).astype(
        jnp.float32
    )
    query_scale = lax.rsqrt(jnp.float32(DH) * positions)
    scaled = (query_rows.astype(jnp.float32) * query_scale[:, None]).astype(jnp.bfloat16)
    shaped = (block_count, BLK, local_heads, DH)
    query_blocks = scaled.reshape(shaped)
    key_blocks = key_rows.reshape(shaped)
    value_blocks = value_rows.reshape(shaped)
    causal = jnp.tril(jnp.ones((BLK, BLK), dtype=bool))
    empty_state = jnp.zeros((local_heads, DH, DH), jnp.float32)
    block_kv = jnp.einsum(
        "bshd,bshe->bhde", key_blocks, value_blocks, preferred_element_type=jnp.float32
    )
    local_total = jnp.sum(block_kv, axis=0)
    earlier = entering(local_total, SEQ, add_states, empty_state, False)
    running_kv = jnp.cumsum(block_kv, axis=0)
    before = earlier[None] + jnp.concatenate([jnp.zeros_like(block_kv), running_kv[:-1]], axis=0)
    inter = jnp.einsum("bthd,bhde->bthe", query_blocks.astype(jnp.float32), before, precision=EXACT)
    scores = jnp.einsum(
        "bthd,bshd->bhts", query_blocks, key_blocks, preferred_element_type=jnp.float32
    )
    scores = jnp.where(causal, scores, 0.0).astype(jnp.bfloat16)
    intra = jnp.einsum("bhts,bshe->bthe", scores, value_blocks, preferred_element_type=jnp.float32)
    attended = (inter + intra).astype(jnp.bfloat16).reshape(rows_dev, feature_width)
    whole_weight = lax.all_gather(out_weight, SEQ, axis=0, tiled=True)
    partial_out = lax.dot_general(
        attended, whole_weight, (((1,), (1,)), ((), ())), preferred_element_type=jnp.float32
    )
    summed = lax.psum_scatter(
        partial_out.astype(jnp.bfloat16), "head", scatter_dimension=1, tiled=True
    )
    residual = (summed.astype(jnp.float32) - target_rows.astype(jnp.float32)).astype(jnp.bfloat16)
    residual_full = lax.all_gather(residual, "head", axis=1, tiled=True)
    grad_attended = jnp.dot(residual_full, whole_weight, preferred_element_type=jnp.float32).astype(
        jnp.bfloat16
    )
    weight_factor = 1.0 / math.sqrt(total_rows)
    product = lax.dot_general(
        residual_full, attended, (((0,), (0,)), ((), ())), preferred_element_type=jnp.float32
    )
    grad_weight = lax.psum_scatter(
        (product * weight_factor).astype(jnp.bfloat16), SEQ, scatter_dimension=0, tiled=True
    ).astype(jnp.float32)
    grad_blocks = grad_attended.reshape(shaped)
    block_qg = jnp.einsum(
        "bthd,bthe->bhde", query_blocks, grad_blocks, preferred_element_type=jnp.float32
    )
    local_grad = jnp.sum(block_qg, axis=0)
    later = entering(local_grad, SEQ, add_states, empty_state, True)
    running_qg = jnp.cumsum(block_qg[::-1], axis=0)[::-1]
    after = later[None] + jnp.concatenate([running_qg[1:], jnp.zeros_like(block_qg)], axis=0)
    mixed = jnp.einsum(
        "bthe,bshe->bhts", grad_blocks, value_blocks, preferred_element_type=jnp.float32
    )
    mixed = jnp.where(causal, mixed, 0.0).astype(jnp.bfloat16)
    grad_scaled = jnp.einsum(
        "bthe,bhde->bthd", grad_blocks.astype(jnp.float32), before, precision=EXACT
    )
    grad_scaled = grad_scaled + jnp.einsum(
        "bhts,bshd->bthd", mixed, key_blocks, preferred_element_type=jnp.float32
    )
    grad_key = jnp.einsum(
        "bshe,bhde->bshd", value_blocks.astype(jnp.float32), after, precision=EXACT
    )
    grad_key = grad_key + jnp.einsum(
        "bhts,bthd->bshd", mixed, query_blocks, preferred_element_type=jnp.float32
    )
    grad_value = jnp.einsum(
        "bshd,bhde->bshe", key_blocks.astype(jnp.float32), after, precision=EXACT
    )
    grad_value = grad_value + jnp.einsum(
        "bhts,bthe->bshe", scores, grad_blocks, preferred_element_type=jnp.float32
    )
    grad_query = (grad_scaled.reshape(rows_dev, feature_width) * query_scale[:, None]).astype(
        jnp.bfloat16
    )
    return (
        summed,
        grad_query,
        grad_key.astype(jnp.bfloat16).reshape(rows_dev, feature_width),
        grad_value.astype(jnp.bfloat16).reshape(rows_dev, feature_width),
        grad_weight,
    )


def solution(mesh):
    torus = Mesh(
        mesh.devices.reshape(4, 4, 2, mesh.shape["head"]), ("seq_0", "seq_1", "seq_2", "head")
    )
    return jax.shard_map(
        on_device,
        mesh=torus,
        in_specs=(P(SEQ, "head"), P(SEQ, "head"), P(SEQ, "head"), P(SEQ, "head"), P(SEQ, "head")),
        out_specs=(P(SEQ, "head"), P(SEQ, "head"), P(SEQ, "head"), P(SEQ, "head"), P(SEQ, "head")),
        check_vma=False,
    )
```

profile of v0, /device:TPU:2, one launch (start us, length us, event | category | flops | bytes accessed | tf_op | source)
XLA Modules:
  0.0 285.8 jit_solution(8579663501388462409)
XLA Ops:
  8.0 1.3 copy.82
  9.3 1.4 multiply_convert_fusion.2
  11.2 2.0 all-gather
  13.3 12.8 %all_gather.31 = bf16[4,4,128,128]{3,2,1,0:T(8,128)(2,1)S(1)} all-gather(bf16[1,4,128,128]{3,2,1,0:T(8,128)(2,1)S(1)} %fusion.41), channel_id=1, replica_groups=mesh['seq_0'=4,'seq_1'=4,'seq_2'=2,'head'=8] {'seq_1'}, dimensions={0}, use_global_device_ids=true | all-gather | bytes 655360 | tf_op jit(solution)/shard_map/all_gather | solution.py:23
  26.2 15.3 %all_gather.32 = bf16[4,4,128,128]{3,2,1,0:T(8,128)(2,1)S(1)} all-gather(bf16[1,4,128,128]{3,2,1,0:T(8,128)(2,1)S(1)} %fusion.40), channel_id=1, replica_groups=mesh['seq_0'=4,'seq_1'=4,'seq_2'=2,'head'=8] {'seq_0'}, dimensions={0}, use_global_device_ids=true | all-gather | bytes 655360 | tf_op jit(solution)/shard_map/all_gather | solution.py:23
  41.8 2.0 select_convert_fusion.1
  44.7 1.4 fusion
  46.1 18.6 %all-gather.5.cloned.1.call-done = bf16[4096,512]{1,0:T(8,128)(2,1)} async-done(((bf16[128,512]{1,0:T(8,128)(2,1)}), bf16[4096,512]{1,0:T(8,128)(2,1)}) %all-gather.5.cloned.1.call-update) | async-done | bytes 4194320 | tf_op jit(solution)/shard_map/all_gather | solution.py:70
  64.7 6.7 %convolution_convert_fusion = bf16[512,4096]{1,0:T(8,128)(2,1)} fusion(bf16[512,512]{0,1:T(8,128)(2,1)} %bitcast.114, bf16[4096,512]{1,0:T(8,128)(2,1)} %all-gather.5.cloned.1.call-done), kind=kOutput, calls=%fused_computation.1 | convolution fusion | flops 2149580800 | bytes 8912896 | tf_op jit(solution)/shard_map/dot_general | solution.py:71
  71.5 55.2 %reduce-scatter.3.cloned.1.call-done = bf16[512,512]{1,0:T(8,128)(2,1)} async-done(((bf16[512,4096]{1,0:T(8,128)(2,1)}), bf16[512,512]{1,0:T(8,128)(2,1)}) %reduce-scatter.3.cloned.1.call-update) | async-done | bytes 524304 | tf_op jit(solution)/shard_map/reduce_scatter | solution.py:74
  126.7 2.1 subtract_convert_fusion
  128.9 53.6 %all-gather.7.cloned.1.call-done = bf16[512,4096]{1,0:T(8,128)(2,1)} async-done(((bf16[512,512]{1,0:T(8,128)(2,1)}), bf16[512,4096]{1,0:T(8,128)(2,1)}) %all-gather.7.cloned.1.call-update) | async-done | bytes 4194320 | tf_op jit(solution)/shard_map/all_gather | solution.py:78
  182.5 6.7 %multiply_convert_fusion = bf16[4096,512]{1,0:T(8,128)(2,1)} fusion(bf16[512,4096]{1,0:T(8,128)(2,1)} %all-gather.7.cloned.1.call-done, bf16[512,512]{0,1:T(8,128)(2,1)} %bitcast.115), kind=kOutput, calls=%fused_computation | convolution fusion | flops 2151677952 | bytes 8912896 | tf_op jit(solution)/shard_map/dot_general | solution.py:83
  189.3 5.8 %convolution_convert_fusion.1 = bf16[512,512]{0,1:T(8,128)(2,1)S(1)} fusion(bf16[512,4096]{1,0:T(8,128)(2,1)} %all-gather.7.cloned.1.call-done, bf16[4096,512]{1,0:T(8,128)(2,1)} %all-gather.5.cloned.1.call-done), kind=kOutput, calls=%fused_computation.10 | convolution fusion | flops 2147745792 | bytes 8912896 | tf_op jit(solution)/shard_map/dot_general | solution.py:79
  195.4 2.1 all-gather.1
  197.6 13.5 %all_gather.36 = bf16[4,4,128,128]{3,2,1,0:T(8,128)(2,1)S(1)} all-gather(bf16[1,4,128,128]{3,2,1,0:T(8,128)(2,1)S(1)} %fusion.42), channel_id=1, replica_groups=mesh['seq_0'=4,'seq_1'=4,'seq_2'=2,'head'=8] {'seq_1'}, dimensions={0}, use_global_device_ids=true | all-gather | bytes 655360 | tf_op jit(solution)/shard_map/all_gather | solution.py:23
  211.2 13.5 %all_gather.37 = bf16[4,4,128,128]{3,2,1,0:T(8,128)(2,1)S(1)} all-gather(bf16[1,4,128,128]{3,2,1,0:T(8,128)(2,1)S(1)} %fusion.39), channel_id=1, replica_groups=mesh['seq_0'=4,'seq_1'=4,'seq_2'=2,'head'=8] {'seq_0'}, dimensions={0}, use_global_device_ids=true | all-gather | bytes 655360 | tf_op jit(solution)/shard_map/all_gather | solution.py:23
  226.0 1.0 copy.49
  227.0 1.9 select_convert_fusion
  229.4 1.4 fusion.1
  230.8 2.1 copy.48
  232.9 1.8 convolution_bitcast_fusion
  236.7 41.0 %reduce-scatter.5.cloned.1.call-done = bf16[128,512]{1,0:T(8,128)(2,1)} async-done(((bf16[4096,512]{1,0:T(8,128)(2,1)}), bf16[128,512]{1,0:T(8,128)(2,1)}) %reduce-scatter.5.cloned.1.call-update) | async-done | bytes 131088 | tf_op jit(solution)/shard_map/reduce_scatter | solution.py:86
  277.6 1.6 convert_element_type.247
  (42 shorter events, 6.7 us)
Async XLA Ops:
  7.2 3.7 %copy-start = (bf16[512,512]{1,0:T(8,128)(2,1)S(1)}, bf16[512,512]{1,0:T(8,128)(2,1)}, u32[]{:S(2)}) copy-start(bf16[512,512]{1,0:T(8,128)(2,1)} %param.7) | copy-start | bytes 1572868
  7.2 57.6 %all-gather.5.cloned.1.call-start = ((), (), s32[]{:S(2)}) async-start(), calls=%async_computation.2 | async-start | bytes 4325376 | tf_op jit(solution)/shard_map/all_gather | solution.py:70
  7.9 118.8 %reduce-scatter.3.cloned.1.call-start = ((), (), s32[]{:S(2)}) async-start(), calls=%async_computation.3 | async-start | bytes 4718592 | tf_op jit(solution)/shard_map/reduce_scatter | solution.py:74
  9.2 32.6 %copy-start.5 = (bf16[512,512]{0,1:T(8,128)(2,1)}, bf16[512,512]{0,1:T(8,128)(2,1)S(1)}, u32[]{:S(2)}) copy-start(bf16[512,512]{0,1:T(8,128)(2,1)S(1)} %copy.82) | copy-start | bytes 1572868
  13.3 31.4 %copy-start.7 = (pred[512,512]{1,0:T(8,128)(4,1)}, pred[512,512]{1,0:T(8,128)(4,1)S(1)}, u32[]{:S(2)}) copy-start(pred[512,512]{1,0:T(8,128)(4,1)S(1)} %iota_compare_fusion) | copy-start | bytes 786436
  41.8 2.8 copy-start.3
  71.5 111.0 %all-gather.7.cloned.1.call-start = ((), (), s32[]{:S(2)}) async-start(), calls=%async_computation.4 | async-start | bytes 4718592 | tf_op jit(solution)/shard_map/all_gather | solution.py:78
  128.9 148.8 %reduce-scatter.5.cloned.1.call-start = ((), (), s32[]{:S(2)}) async-start(), calls=%async_computation.5 | async-start | bytes 4325376 | tf_op jit(solution)/shard_map/reduce_scatter | solution.py:86
  195.1 30.3 %copy-start.1 = (bf16[512,512]{0,1:T(8,128)(2,1)}, bf16[512,512]{0,1:T(8,128)(2,1)S(1)}, u32[]{:S(2)}) copy-start(bf16[512,512]{0,1:T(8,128)(2,1)S(1)} %convolution_convert_fusion.1) | copy-start | bytes 1572868
  195.4 30.0 %copy-start.6 = (bf16[512,512]{1,0:T(8,128)(2,1)S(1)}, bf16[512,512]{1,0:T(8,128)(2,1)}, u32[]{:S(2)}) copy-start(bf16[512,512]{1,0:T(8,128)(2,1)} %param.6) | copy-start | bytes 1572868
  229.4 5.3 %copy-start.2 = (bf16[512,512]{0,1:T(8,128)(2,1)S(1)}, bf16[512,512]{0,1:T(8,128)(2,1)}, u32[]{:S(2)}) copy-start(bf16[512,512]{0,1:T(8,128)(2,1)} %copy-done.1) | copy-start | bytes 1572868
  230.8 4.0 %copy-start.4 = (f32[4,128,128]{2,1,0:T(8,128)S(1)}, f32[4,128,128]{2,1,0:T(8,128)}, u32[]{:S(2)}) copy-start(f32[4,128,128]{2,1,0:T(8,128)} %copy-done.3) | copy-start | bytes 786436
Sparse Core Ops, SparseCore 0:
  10.5 54.1 all-gather.4
  71.6 55.0 reduce-scatter.2
  129.1 53.3 all-gather.6
  189.3 88.2 reduce-scatter.4
where the time goes:
time: 286 us
  waiting for transfers between devices  169 us (59%)
  blocking collectives  59.3 us (21%)
  matrix products  31.3 us (11%)
  between operations  14.1 us (5%)
  other arithmetic  6.88 us (2%)
  local copies, waits for them, and re-layouts  4.94 us (2%)
    all_gather x6, blocking collectives, entering(): pieces = lax.all_gather(so_far.astype(jnp.bfloat16), axis)  59.3 us
    reduce_scatter x1, waiting for transfers between devices, on_device(): lax.psum_scatter(partial_out.astype(jnp.bfloat16), 'head', scatter_dimens...  55.2 us
    all_gather x1, waiting for transfers between devices, on_device(): residual_full = lax.all_gather(residual, 'head', axis=1, tiled=True)  53.6 us
    reduce_scatter x1, waiting for transfers between devices, on_device(): lax.psum_scatter((product * weight_factor).astype(jnp.bfloat16), SEQ, sca...  41 us
    all_gather x1, waiting for transfers between devices, on_device(): whole_weight = lax.all_gather(out_weight, SEQ, axis=0, tiled=True)  18.6 us
    dot_general x1, matrix products, on_device(): lax.dot_general(attended, whole_weight, (((1,), (1,)), ((), ())), preferr...  6.73 us
    dot_general x1, matrix products, on_device(): lax.dot_general(residual_full, attended, (((0,), (0,)), ((), ())), prefer...  6.68 us
    dot_general x1, matrix products, on_device(): jnp.dot(residual_full, whole_weight, preferred_element_type=jnp.float32)  5.84 us
  transfers between devices with their start and end apart: 4, of which 4 were waited for; matrix products, arithmetic and copies ran while one was open for 9% of the time, Pallas kernels for 0%

commit v1 on v0

--- a/solution.py
+++ b/solution.py
@@ -75,7 +75,14 @@
         partial_out.astype(jnp.bfloat16), "head", scatter_dimension=1, tiled=True
     )
     residual = (summed.astype(jnp.float32) - target_rows.astype(jnp.float32)).astype(jnp.bfloat16)
-    residual_full = lax.all_gather(residual, "head", axis=1, tiled=True)
+    peers = lax.axis_size("head")
+    right = [(i, (i + 1) % peers) for i in range(peers)]
+    parts = [residual]
+    for hop in range(1, peers):
+        parts = [lax.ppermute(parts[0], "head", right), *parts]
+    full = jnp.concatenate(parts, axis=1)
+    shift = (lax.axis_index("head") + 1) * parts[-1].shape[1]
+    residual_full = jnp.roll(full, shift, axis=1)
     grad_attended = jnp.dot(residual_full, whole_weight, preferred_element_type=jnp.float32).astype(
         jnp.bfloat16
     )

time: 286 us -> 338 us (1.18)
  waiting for transfers between devices: 169 us -> 204 us
  local copies, waits for them, and re-layouts: 4.94 us -> 23.4 us
    ppermute x0 -> x7, waiting for transfers between devices: none -> 87.9 us  [on_device(): parts = [lax.ppermute(parts[0], 'head', right), *parts]]
    all_gather x1 -> x0, waiting for transfers between devices: 53.6 us -> none  [on_device(): residual_full = lax.all_gather(residual, 'head', axis=1, tiled=True)]
    unnamed x18 -> x57, local copies, waits for them, and re-layouts: 3.14 us -> 21.6 us
  transfers between devices with their start and end apart: 4 -> 10, of which waited for: 4 -> 10; matrix products, arithmetic and copies ran while one was open for 9% -> 7% of each run, Pallas kernels for 0% -> 0%
where the time goes in v1:
time: 338 us; the launch traced here: 337 us
  waiting for transfers between devices  204 us (60%)
  blocking collectives  59.1 us (17%)
  matrix products  29.3 us (9%)
  local copies, waits for them, and re-layouts  23.4 us (7%)
  between operations  14.3 us (4%)
  other arithmetic  6.09 us (2%)
    ppermute x7, waiting for transfers between devices, on_device(): parts = [lax.ppermute(parts[0], 'head', right), *parts]  87.9 us
    all_gather x6, blocking collectives, entering(): pieces = lax.all_gather(so_far.astype(jnp.bfloat16), axis)  59.1 us
    reduce_scatter x1, waiting for transfers between devices, on_device(): lax.psum_scatter(partial_out.astype(jnp.bfloat16), 'head', scatter_dimens...  55.2 us
    reduce_scatter x1, waiting for transfers between devices, on_device(): lax.psum_scatter((product * weight_factor).astype(jnp.bfloat16), SEQ, sca...  42 us
    unnamed x57, local copies, waits for them, and re-layouts  21.6 us
    all_gather x1, waiting for transfers between devices, on_device(): whole_weight = lax.all_gather(out_weight, SEQ, axis=0, tiled=True)  18.7 us
  transfers between devices with their start and end apart: 10, of which 10 were waited for; matrix products, arithmetic and copies ran while one was open for 7% of the time, Pallas kernels for 0%

profile of v1, /device:TPU:2, one launch (start us, length us, event | category | flops | bytes accessed | tf_op | source)
XLA Modules:
  0.0 336.8 jit_solution(2920218646783849766)
XLA Ops:
  11.2 2.0 all-gather
  13.3 12.8 %all_gather.28 = bf16[4,4,128,128]{3,2,1,0:T(8,128)(2,1)S(1)} all-gather(bf16[1,4,128,128]{3,2,1,0:T(8,128)(2,1)S(1)} %fusion.47), channel_id=1, replica_groups=mesh['seq_0'=4,'seq_1'=4,'seq_2'=2,'head'=8] {'seq_1'}, dimensions={0}, use_global_device_ids=true | all-gather | bytes 655360 | tf_op jit(solution)/shard_map/all_gather | solution.py:23
  26.3 15.3 %all_gather.29 = bf16[4,4,128,128]{3,2,1,0:T(8,128)(2,1)S(1)} all-gather(bf16[1,4,128,128]{3,2,1,0:T(8,128)(2,1)S(1)} %fusion.46), channel_id=1, replica_groups=mesh['seq_0'=4,'seq_1'=4,'seq_2'=2,'head'=8] {'seq_0'}, dimensions={0}, use_global_device_ids=true | all-gather | bytes 655360 | tf_op jit(solution)/shard_map/all_gather | solution.py:23
  41.8 2.0 select_convert_fusion.1
  46.1 18.7 %all-gather.4.cloned.1.call-done = bf16[4096,512]{1,0:T(8,128)(2,1)} async-done(((bf16[128,512]{1,0:T(8,128)(2,1)}), bf16[4096,512]{1,0:T(8,128)(2,1)}) %all-gather.4.cloned.1.call-update) | async-done | bytes 4194320 | tf_op jit(solution)/shard_map/all_gather | solution.py:70
  64.8 6.7 %convolution_convert_fusion = bf16[512,4096]{1,0:T(8,128)(2,1)} fusion(bf16[512,512]{0,1:T(8,128)(2,1)} %bitcast.112, bf16[4096,512]{1,0:T(8,128)(2,1)} %all-gather.4.cloned.1.call-done), kind=kOutput, calls=%fused_computation.1 | convolution fusion | flops 2149580800 | bytes 8912896 | tf_op jit(solution)/shard_map/dot_general | solution.py:71
  71.6 55.2 %reduce-scatter.3.cloned.1.call-done = bf16[512,512]{1,0:T(8,128)(2,1)} async-done(((bf16[512,4096]{1,0:T(8,128)(2,1)}), bf16[512,512]{1,0:T(8,128)(2,1)}) %reduce-scatter.3.cloned.1.call-update) | async-done | bytes 524304 | tf_op jit(solution)/shard_map/reduce_scatter | solution.py:74
  129.0 14.8 %collective-permute-done = bf16[512,512]{1,0:T(8,128)(2,1)S(1)} collective-permute-done((bf16[512,512]{1,0:T(8,128)(2,1)S(1)}, bf16[512,512]{1,0:T(8,128)(2,1)S(1)}, u32[]{:S(2)}, u32[]{:S(2)}) %collective-permute-start) | collective-permute-done | bytes 524320 | tf_op jit(solution)/shard_map/ppermute | solution.py:82
  144.5 13.9 %collective-permute-done.1 = bf16[512,512]{1,0:T(8,128)(2,1)S(1)} collective-permute-done((bf16[512,512]{1,0:T(8,128)(2,1)S(1)}, bf16[512,512]{1,0:T(8,128)(2,1)S(1)}, u32[]{:S(2)}, u32[]{:S(2)}) %collective-permute-start.1) | collective-permute-done | bytes 524320 | tf_op jit(solution)/shard_map/ppermute | solution.py:82
  159.3 13.1 %collective-permute-done.2 = bf16[512,512]{1,0:T(8,128)(2,1)S(1)} collective-permute-done((bf16[512,512]{1,0:T(8,128)(2,1)S(1)}, bf16[512,512]{1,0:T(8,128)(2,1)S(1)}, u32[]{:S(2)}, u32[]{:S(2)}) %collective-permute-start.2) | collective-permute-done | bytes 524320 | tf_op jit(solution)/shard_map/ppermute | solution.py:82
  173.2 12.2 %collective-permute-done.3 = bf16[512,512]{1,0:T(8,128)(2,1)S(1)} collective-permute-done((bf16[512,512]{1,0:T(8,128)(2,1)S(1)}, bf16[512,512]{1,0:T(8,128)(2,1)S(1)}, u32[]{:S(2)}, u32[]{:S(2)}) %collective-permute-start.3) | collective-permute-done | bytes 524320 | tf_op jit(solution)/shard_map/ppermute | solution.py:82
  186.2 11.4 %collective-permute-done.4 = bf16[512,512]{1,0:T(8,128)(2,1)S(1)} collective-permute-done((bf16[512,512]{1,0:T(8,128)(2,1)S(1)}, bf16[512,512]{1,0:T(8,128)(2,1)S(1)}, u32[]{:S(2)}, u32[]{:S(2)}) %collective-permute-start.4) | collective-permute-done | bytes 524320 | tf_op jit(solution)/shard_map/ppermute | solution.py:82
  198.3 11.9 %collective-permute-done.5 = bf16[512,512]{1,0:T(8,128)(2,1)} collective-permute-done((bf16[512,512]{1,0:T(8,128)(2,1)S(1)}, bf16[512,512]{1,0:T(8,128)(2,1)}, u32[]{:S(2)}, u32[]{:S(2)}) %collective-permute-start.5) | collective-permute-done | bytes 524320 | tf_op jit(solution)/shard_map/ppermute | solution.py:82
  210.3 10.6 %collective-permute-done.6 = bf16[512,512]{1,0:T(8,128)(2,1)} collective-permute-done((bf16[512,512]{1,0:T(8,128)(2,1)}, bf16[512,512]{1,0:T(8,128)(2,1)}, u32[]{:S(2)}, u32[]{:S(2)}) %collective-permute-start.6) | collective-permute-done | bytes 524320 | tf_op jit(solution)/shard_map/ppermute | solution.py:82
  232.5 3.3 copy-done.19
  235.8 4.4 %multiply_convert_fusion = bf16[4096,512]{1,0:T(8,128)(2,1)} fusion(bf16[512,512]{0,1:T(8,128)(2,1)S(1)} %bitcast.113, bf16[512,8192]{1,0:T(8,128)(2,1)S(1)} %constant_dynamic-update-slice_fusion, s32[]{:T(128)S(6)} %select_n.188), kind=kOutput, calls=%fused_computation | convolution fusion | flops 2151677952 | bytes 8912900 | tf_op jit(solution)/shard_map/dot_general | solution.py:90
  240.2 5.8 %fusion.3 = bf16[512,512]{0,1:T(8,128)(2,1)S(1)} fusion(bf16[4096,512]{1,0:T(8,128)(2,1)} %all-gather.4.cloned.1.call-done, bf16[512,8192]{1,0:T(8,128)(2,1)} %copy-done.19, s32[]{:T(128)S(6)} %select_n.188), kind=kOutput, calls=%fused_computation.13 | convolution fusion | flops 2147745792 | bytes 8912900 | tf_op jit(solution)/shard_map/dot_general | solution.py:86
  246.4 2.1 all-gather.1
  248.6 13.6 %all_gather.32 = bf16[4,4,128,128]{3,2,1,0:T(8,128)(2,1)S(1)} all-gather(bf16[1,4,128,128]{3,2,1,0:T(8,128)(2,1)S(1)} %fusion.48), channel_id=1, replica_groups=mesh['seq_0'=4,'seq_1'=4,'seq_2'=2,'head'=8] {'seq_1'}, dimensions={0}, use_global_device_ids=true | all-gather | bytes 655360 | tf_op jit(solution)/shard_map/all_gather | solution.py:23
  262.2 13.2 %all_gather.33 = bf16[4,4,128,128]{3,2,1,0:T(8,128)(2,1)S(1)} all-gather(bf16[1,4,128,128]{3,2,1,0:T(8,128)(2,1)S(1)} %fusion.45), channel_id=1, replica_groups=mesh['seq_0'=4,'seq_1'=4,'seq_2'=2,'head'=8] {'seq_0'}, dimensions={0}, use_global_device_ids=true | all-gather | bytes 655360 | tf_op jit(solution)/shard_map/all_gather | solution.py:23
  277.8 1.9 select_convert_fusion
  281.8 1.8 convolution_bitcast_fusion
  283.7 1.7 convolution_add_fusion.2
  286.7 42.0 %reduce-scatter.5.cloned.1.call-done = bf16[128,512]{1,0:T(8,128)(2,1)} async-done(((bf16[4096,512]{1,0:T(8,128)(2,1)}), bf16[128,512]{1,0:T(8,128)(2,1)}) %reduce-scatter.5.cloned.1.call-update) | async-done | bytes 131088 | tf_op jit(solution)/shard_map/reduce_scatter | solution.py:93
  (93 shorter events, 32.0 us)
Async XLA Ops:
  7.2 3.7 %copy-start = (bf16[512,512]{1,0:T(8,128)(2,1)S(1)}, bf16[512,512]{1,0:T(8,128)(2,1)}, u32[]{:S(2)}) copy-start(bf16[512,512]{1,0:T(8,128)(2,1)} %param.7) | copy-start | bytes 1572868
  7.2 57.6 %all-gather.4.cloned.1.call-start = ((), (), s32[]{:S(2)}) async-start(), calls=%async_computation.2 | async-start | bytes 4325376 | tf_op jit(solution)/shard_map/all_gather | solution.py:70
  7.9 118.8 %reduce-scatter.3.cloned.1.call-start = ((), (), s32[]{:S(2)}) async-start(), calls=%async_computation.3 | async-start | bytes 4718592 | tf_op jit(solution)/shard_map/reduce_scatter | solution.py:74
  9.2 1.6 copy-start.5
  13.3 28.6 %copy-start.18 = (pred[512,512]{1,0:T(8,128)(4,1)}, pred[512,512]{1,0:T(8,128)(4,1)S(1)}, u32[]{:S(2)}) copy-start(pred[512,512]{1,0:T(8,128)(4,1)S(1)} %iota_compare_fusion) | copy-start | bytes 786436
  41.8 2.8 copy-start.4
  71.5 257.2 %reduce-scatter.5.cloned.1.call-start = ((), (), s32[]{:S(2)}) async-start(), calls=%async_computation.4 | async-start | bytes 4325376 | tf_op jit(solution)/shard_map/reduce_scatter | solution.py:93
  129.0 14.8 %collective-permute-start = (bf16[512,512]{1,0:T(8,128)(2,1)S(1)}, bf16[512,512]{1,0:T(8,128)(2,1)S(1)}, u32[]{:S(2)}, u32[]{:S(2)}) collective-permute-start(bf16[512,512]{1,0:T(8,128)(2,1)S(1)} %subtract_convert_fusion), channel_id=1, source_target_pairs={{0,1},{1,2},{2,3},{3,4},{4,5},{5,6},{6,7},{7,0},{8,9},{9,10},{10,1... | collective-permute-start | bytes 1572872 | tf_op jit(solution)/shard_map/ppermute | solution.py:82
  144.5 13.9 %collective-permute-start.1 = (bf16[512,512]{1,0:T(8,128)(2,1)S(1)}, bf16[512,512]{1,0:T(8,128)(2,1)S(1)}, u32[]{:S(2)}, u32[]{:S(2)}) collective-permute-start(bf16[512,512]{1,0:T(8,128)(2,1)S(1)} %collective-permute-done), channel_id=1, source_target_pairs={{0,1},{1,2},{2,3},{3,4},{4,5},{5,6},{6,7},{7,0},{8,9},{9,10},{10,1... | collective-permute-start | bytes 1572872 | tf_op jit(solution)/shard_map/ppermute | solution.py:82
  159.3 13.1 %collective-permute-start.2 = (bf16[512,512]{1,0:T(8,128)(2,1)S(1)}, bf16[512,512]{1,0:T(8,128)(2,1)S(1)}, u32[]{:S(2)}, u32[]{:S(2)}) collective-permute-start(bf16[512,512]{1,0:T(8,128)(2,1)S(1)} %collective-permute-done.1), channel_id=1, source_target_pairs={{0,1},{1,2},{2,3},{3,4},{4,5},{5,6},{6,7},{7,0},{8,9},{9,10},{10,1... | collective-permute-start | bytes 1572872 | tf_op jit(solution)/shard_map/ppermute | solution.py:82
  173.2 12.2 %collective-permute-start.3 = (bf16[512,512]{1,0:T(8,128)(2,1)S(1)}, bf16[512,512]{1,0:T(8,128)(2,1)S(1)}, u32[]{:S(2)}, u32[]{:S(2)}) collective-permute-start(bf16[512,512]{1,0:T(8,128)(2,1)S(1)} %collective-permute-done.2), channel_id=1, source_target_pairs={{0,1},{1,2},{2,3},{3,4},{4,5},{5,6},{6,7},{7,0},{8,9},{9,10},{10,1... | collective-permute-start | bytes 1572872 | tf_op jit(solution)/shard_map/ppermute | solution.py:82
  186.2 11.4 %collective-permute-start.4 = (bf16[512,512]{1,0:T(8,128)(2,1)S(1)}, bf16[512,512]{1,0:T(8,128)(2,1)S(1)}, u32[]{:S(2)}, u32[]{:S(2)}) collective-permute-start(bf16[512,512]{1,0:T(8,128)(2,1)S(1)} %collective-permute-done.3), channel_id=1, source_target_pairs={{0,1},{1,2},{2,3},{3,4},{4,5},{5,6},{6,7},{7,0},{8,9},{9,10},{10,1... | collective-permute-start | bytes 1572872 | tf_op jit(solution)/shard_map/ppermute | solution.py:82
  198.3 11.9 %collective-permute-start.5 = (bf16[512,512]{1,0:T(8,128)(2,1)S(1)}, bf16[512,512]{1,0:T(8,128)(2,1)}, u32[]{:S(2)}, u32[]{:S(2)}) collective-permute-start(bf16[512,512]{1,0:T(8,128)(2,1)S(1)} %collective-permute-done.4), channel_id=1, source_target_pairs={{0,1},{1,2},{2,3},{3,4},{4,5},{5,6},{6,7},{7,0},{8,9},{9,10},{10,1... | collective-permute-start | bytes 1572872 | tf_op jit(solution)/shard_map/ppermute | solution.py:82
  210.2 10.7 %collective-permute-start.6 = (bf16[512,512]{1,0:T(8,128)(2,1)}, bf16[512,512]{1,0:T(8,128)(2,1)}, u32[]{:S(2)}, u32[]{:S(2)}) collective-permute-start(bf16[512,512]{1,0:T(8,128)(2,1)} %collective-permute-done.5), channel_id=1, source_target_pairs={{0,1},{1,2},{2,3},{3,4},{4,5},{5,6},{6,7},{7,0},{8,9},{9,10},{10,1... | collective-permute-start | bytes 1572872 | tf_op jit(solution)/shard_map/ppermute | solution.py:82
  210.2 21.9 %copy-start.15 = (bf16[512,512]{1,0:T(8,128)(2,1)S(1)}, bf16[512,512]{1,0:T(8,128)(2,1)}, u32[]{:S(2)}) copy-start(bf16[512,512]{1,0:T(8,128)(2,1)} %copy-done.14) | copy-start | bytes 1572868
  210.2 22.0 %copy-start.13 = (bf16[512,512]{1,0:T(8,128)(2,1)S(1)}, bf16[512,512]{1,0:T(8,128)(2,1)}, u32[]{:S(2)}) copy-start(bf16[512,512]{1,0:T(8,128)(2,1)} %copy-done.12) | copy-start | bytes 1572868
  210.2 22.0 %copy-start.11 = (bf16[512,512]{1,0:T(8,128)(2,1)S(1)}, bf16[512,512]{1,0:T(8,128)(2,1)}, u32[]{:S(2)}) copy-start(bf16[512,512]{1,0:T(8,128)(2,1)} %copy-done.10) | copy-start | bytes 1572868
  210.2 22.1 %copy-start.9 = (bf16[512,512]{1,0:T(8,128)(2,1)S(1)}, bf16[512,512]{1,0:T(8,128)(2,1)}, u32[]{:S(2)}) copy-start(bf16[512,512]{1,0:T(8,128)(2,1)} %copy-done.8) | copy-start | bytes 1572868
  210.2 22.1 %copy-start.7 = (bf16[512,512]{1,0:T(8,128)(2,1)S(1)}, bf16[512,512]{1,0:T(8,128)(2,1)}, u32[]{:S(2)}) copy-start(bf16[512,512]{1,0:T(8,128)(2,1)} %copy-done.6) | copy-start | bytes 1572868
  210.2 22.2 %copy-start.2 = (bf16[512,512]{1,0:T(8,128)(2,1)S(1)}, bf16[512,512]{1,0:T(8,128)(2,1)}, u32[]{:S(2)}) copy-start(bf16[512,512]{1,0:T(8,128)(2,1)} %copy-done.1) | copy-start | bytes 1572868
  210.2 25.5 %copy-start.17 = (bf16[4,128,512]{2,1,0:T(8,128)(2,1)S(1)}, bf16[4,128,512]{2,1,0:T(8,128)(2,1)}, u32[]{:S(2)}) copy-start(bf16[4,128,512]{2,1,0:T(8,128)(2,1)} %fusion.6) | copy-start | bytes 1572868
  232.5 3.3 copy-start.19
  246.1 30.1 %copy-start.3 = (bf16[512,512]{0,1:T(8,128)(2,1)}, bf16[512,512]{0,1:T(8,128)(2,1)S(1)}, u32[]{:S(2)}) copy-start(bf16[512,512]{0,1:T(8,128)(2,1)S(1)} %fusion.3) | copy-start | bytes 1572868
  246.1 30.1 %copy-start.16 = (bf16[512,512]{1,0:T(8,128)(2,1)S(1)}, bf16[512,512]{1,0:T(8,128)(2,1)}, u32[]{:S(2)}) copy-start(bf16[512,512]{1,0:T(8,128)(2,1)} %param.6) | copy-start | bytes 1572868
  (6 other events, 4.9 us)
Sparse Core Ops, SparseCore 0:
  10.5 54.1 all-gather.3
  71.6 55.0 reduce-scatter.2
  240.3 88.3 reduce-scatter.4
